TPU v7x, 32 devices: a whole 2x2x4 slice. The times are simulated.
32 devices in a mesh: grp: 2 (over x), seq: 8 (over z, y), head: 2 (over core).
Axes of the slice: x: 2, y: 2, z: 4, core: 2. Of those that a mesh axis runs over, the one named last changes fastest.
Arguments:
- q_feat: bfloat16 [8192, 256], P(('grp', 'seq'), 'head'), parts along dimension 0, may hold values from -5 to 5
- k_feat: bfloat16 [8192, 256], P(('grp', 'seq'), 'head'), parts along dimension 0, may hold values from -5 to 5
- values: bfloat16 [8192, 2048], P(('grp', 'seq'), 'head'), parts along dimension 0, may hold values from -8 to 8
- win_query: bfloat16 [8192, 2048], P(('grp', 'seq'), 'head'), parts along dimension 0, may hold values from -20 to 20
- win_key: bfloat16 [8192, 2048], P(('grp', 'seq'), 'head'), parts along dimension 0, may hold values from -5 to 5
- log_gates: float32 [8192, 16], P(('grp', 'seq'), 'head'), parts along dimension 0, may hold values from -2.2 to 0
- conv_weight: float32 [3, 2048], P(None, 'head'), may hold values from -2.5 to 2.5
Outputs:
- mixed: bfloat16 [8192, 2048], P(('grp', 'seq'), 'head'), parts along dimension 0
There are 2 independent parts, one for each index of `grp`. A program takes and returns all parts, laid end to end along the dimension named above; an argument that names none is the same for every part. Nothing has to cross between parts.
All inputs are finite; a program needn't handle non-finite values.
Results may differ from a plain program's by a relative error of at most 0.011.
Values may be sent and summed in bfloat16 or wider, within the bound.
A program may use at most 192 MiB of HBM per device.

v0:
```python
import jax
import jax.numpy as jnp
from jax import lax
from jax.sharding import PartitionSpec as P

WINDOW = 64
BLOCK = 512


def passed_along(block, axis, distance):
    devices = range(lax.axis_size(axis))
    route = [(i - distance, i) for i in devices if i - distance in devices]
    return lax.ppermute(block, axis, route)


def prefix(value, axis, join, neutral):
    count, mine = (lax.axis_size(axis), lax.axis_index(axis))
    pieces = jax.tree.map(lambda part: lax.all_gather(part, axis), value)
    so_far = jax.tree.map(
        lambda part, zero: jnp.full_like(part, 0) + jnp.asarray(zero, part.dtype), value, neutral
    )

    def hop(position, so_far):
        longer = join(so_far, jax.tree.map(lambda part: part[position], pieces))
        return jax.tree.map(lambda new, old: jnp.where(position < mine, new, old), longer, so_far)

    return lax.fori_loop(0, count - 1, hop, so_far)


def taylor_map(features, heads):
    tok_rows = features.shape[0]
    width = features.shape[1] // heads
    spread = features.astype(jnp.float32).reshape(tok_rows, heads, width)
    linear = spread * width ** (-0.25)
    square = (spread[:, :, :, None] * spread[:, :, None, :]).reshape(
        tok_rows, heads, width * width
    ) * (2.0 * width) ** (-0.5)
    ones = jnp.ones((tok_rows, heads, 1), jnp.float32)
    return jnp.concatenate([ones, linear, square], axis=2).astype(jnp.bfloat16)


def three_parts(wide):
    upper = wide.astype(jnp.bfloat16)
    remain = wide - upper.astype(jnp.float32)
    middle = remain.astype(jnp.bfloat16)
    lowest = (remain - middle.astype(jnp.float32)).astype(jnp.bfloat16)
    return (upper, middle, lowest)


def divided_product(form, narrow, wide):
    total = None
    for piece in three_parts(wide):
        term = jnp.einsum(form, narrow, piece, preferred_element_type=jnp.float32)
        total = term if total is None else total + term
    return total


def combine_states(earlier, later):
    decay_a, state_a, norm_a = earlier
    decay_b, state_b, norm_b = later
    return (
        decay_a * decay_b,
        decay_b[:, None, None] * state_a + state_b,
        decay_b[:, None] * norm_a + norm_b,
    )


def local(q_feat, k_feat, values, win_query, win_key, log_gates, conv_weight):
    seq_rows = values.shape[0]
    heads_here = log_gates.shape[1]
    head_size = values.shape[1] // heads_here
    feat_width = q_feat.shape[1] // heads_here
    features = 1 + feat_width + feat_width * feat_width
    block = BLOCK
    window = WINDOW
    prev_key, prev_value = passed_along(
        (win_key[seq_rows - window :], values[seq_rows - window :]), "seq", 1
    )
    value_ext = jnp.concatenate([prev_value, values], axis=0)
    key_ext = jnp.concatenate([prev_key, win_key], axis=0)
    convolved = jnp.zeros(values.shape, jnp.float32)
    for tap in range(conv_weight.shape[0]):
        convolved = convolved + conv_weight[tap][None, :] * value_ext[
            window - tap : window - tap + seq_rows
        ].astype(jnp.float32)
    filtered_values = convolved.astype(jnp.bfloat16).reshape(seq_rows, heads_here, head_size)
    query_features = taylor_map(q_feat, heads_here)
    key_features = taylor_map(k_feat, heads_here)
    device_start = lax.axis_index("seq") * seq_rows
    causal = jnp.arange(block)[:, None] >= jnp.arange(block)[None, :]
    running_state = jnp.zeros((heads_here, features, head_size), jnp.float32)
    norm_total = jnp.zeros((heads_here, features), jnp.float32)
    cumulative = jnp.cumsum(log_gates, axis=0)
    cum_heads = cumulative.T
    decay_factor = jnp.exp(
        jnp.where(causal[None], cum_heads[:, :, None] - cum_heads[:, None, :], -jnp.inf)
    )
    score_matrix = (
        jnp.einsum("sjz,djz->jsd", query_features, key_features, preferred_element_type=jnp.float32)
        * decay_factor
    )
    den_block = jnp.sum(score_matrix, axis=2).T
    num_block = jnp.einsum(
        "hqk,khd->qhd",
        score_matrix.astype(jnp.bfloat16),
        filtered_values,
        preferred_element_type=jnp.float32,
    )
    block_finish = cumulative[-1]
    retention = jnp.exp(block_finish[None, :] - cumulative)
    weighted_values = filtered_values.astype(jnp.float32) * retention[:, :, None]
    running_state = jnp.exp(block_finish)[:, None, None] * running_state + divided_product(
        "mwv,mwr->wvr", key_features, weighted_values
    )
    norm_total = jnp.exp(block_finish)[:, None] * norm_total + divided_product(
        "vin,vi->in", key_features, retention
    )
    decay_parts = jnp.exp(cumulative)
    win_keys = key_ext.reshape(block + window, heads_here, head_size)
    win_values = value_ext.reshape(block + window, heads_here, head_size)
    win_queries = win_query.reshape(block, heads_here, head_size)
    win_scores = jnp.einsum(
        "qhd,khd->hqk", win_queries, win_keys, preferred_element_type=jnp.float32
    ) * head_size ** (-0.5)
    key_pos = 0 - window + jnp.arange(block + window)
    query_pos = 0 + jnp.arange(block)
    valid = (
        (key_pos[None, :] <= query_pos[:, None])
        & (key_pos[None, :] > query_pos[:, None] - window)
        & (device_start + key_pos[None, :] >= 0)
    )
    win_scores = jnp.where(valid[None], win_scores, -jnp.inf)
    top = jnp.max(win_scores, axis=2, keepdims=True)
    weights = jnp.exp(win_scores - top)
    total = jnp.sum(weights, axis=2, keepdims=True)
    probs = (weights / total).astype(jnp.bfloat16)
    window_parts = jnp.einsum("hqk,khd->qhd", probs, win_values, preferred_element_type=jnp.float32)
    numerator = num_block
    denominator = den_block
    decay_total = jnp.exp(block_finish)
    identity = (
        jnp.ones_like(decay_total),
        jnp.zeros_like(running_state),
        jnp.zeros_like(norm_total),
    )
    carried = prefix((decay_total, running_state, norm_total), "seq", combine_states, identity)
    prefix_state = carried[1]
    prefix_norm = carried[2]
    numerator = numerator + decay_parts[:, :, None] * divided_product(
        "thf,hfd->thd", query_features, prefix_state
    )
    denominator = denominator + decay_parts * divided_product(
        "thf,hf->th", query_features, prefix_norm
    )
    mixed = numerator / denominator[:, :, None] + window_parts
    return mixed.astype(jnp.bfloat16).reshape(seq_rows, heads_here * head_size)


def solution(mesh):
    placed = (
        P(("grp", "seq"), "head"),
        P(("grp", "seq"), "head"),
        P(("grp", "seq"), "head"),
        P(("grp", "seq"), "head"),
        P(("grp", "seq"), "head"),
        P(("grp", "seq"), "head"),
        P(None, "head"),
    )
    return jax.shard_map(
        local, mesh=mesh, in_specs=placed, out_specs=P(("grp", "seq"), "head"), check_vma=False
    )
```

profile of v0, /device:TPU:0, one launch (start us, length us, event | category | flops | bytes accessed | tf_op | source)
XLA Modules:
  0.0 220.2 jit_solution(10231950504331805521)
XLA Ops:
  6.5 1.7 slice.32
  8.2 5.5 %collective-permute-start = (bf16[64,1024]{1,0:T(8,128)(2,1)}, bf16[64,1024]{1,0:T(8,128)(2,1)}, u32[]{:S(2)}, u32[]{:S(2)}) collective-permute-start(bf16[64,1024]{1,0:T(8,128)(2,1)} %slice.32), channel_id=1, source_target_pairs={{0,2},{2,4},{4,6},{6,8},{8,10},{10,12},{12,14},{1,3},{3,5},{5,7},{... | collective-permute-start | bytes 393224 | tf_op jit(solution)/shard_map/ppermute | solution.py:13
  13.7 1.0 copy.39
  14.7 2.0 multiply_convert_fusion
  16.7 0.1 copy.38
  16.8 0.7 multiply_convert_fusion.2
  17.5 2.0 multiply_convert_fusion.1
  19.5 1.1 reduce-window.6
  20.6 0.2 slice_reduce_fusion
  20.8 0.1 fusion.89
  20.9 0.2 slice_reduce_fusion.1
  21.1 0.1 convert_bitcast_fusion
  21.2 3.3 %pad_maximum_fusion.1 = (bf16[512,8,273]{0,2,1:T(8,128)(2,1)S(1)}, bf16[512,8,273]{0,2,1:T(8,128)(2,1)S(1)}) fusion(bf16[512,8,256]{0,2,1:T(8,128)(2,1)} %bitcast.155, bf16[512,8,16]{0,2,1:T(8,128)(2,1)S(1)} %get-tuple-element.197, bf16[273]{0:T(512)(128)(2,1)S(1)} %pad.5.clone, bf16[512,8,256]{0,2,1:T(8,128)(2,1)} %bitcast.156, ...), kind=kLoop, calls=%fused_computation.28 | loop fusion | flops 12300288 | bytes 8929826 | tf_op jit(solution)/shard_map/concatenate | solution.py:39
  24.6 1.1 constant_dynamic-update-slice_fusion.1
  25.7 0.8 fusion.45
  26.6 1.2 fusion.46
  27.8 1.2 fusion.36
  29.1 1.3 fusion.33
  30.4 1.2 copy.43
  31.6 1.6 slice.39
  33.1 3.4 %collective-permute-start.1 = (bf16[64,1024]{1,0:T(8,128)(2,1)}, bf16[64,1024]{1,0:T(8,128)(2,1)}, u32[]{:S(2)}, u32[]{:S(2)}) collective-permute-start(bf16[64,1024]{1,0:T(8,128)(2,1)} %slice.39), channel_id=1, source_target_pairs={{0,2},{2,4},{4,6},{6,8},{8,10},{10,12},{12,14},{1,3},{3,5},{5,7},{... | collective-permute-start | bytes 393224 | tf_op jit(solution)/shard_map/ppermute | solution.py:13
  36.6 0.1 iota_compare_fusion.1
  36.7 0.1 add_bitcast_fusion.1
  36.8 1.1 fusion.44
  37.8 2.6 %fusion.67 = f32[8,1,273]{2,1,0:T(1,128)S(1)} fusion(bf16[512,8,273]{0,2,1:T(8,128)(2,1)} %copy-done.3, bf16[512,8,1]{0,1,2:T(8,128)(2,1)S(1)} %get-tuple-element.184), kind=kOutput, calls=%fused_computation.84 | convolution fusion | flops 2236416 | bytes 2253344 | tf_op jit(solution)/shard_map/vin,vi->in/dot_general | solution.py:53
  40.4 0.7 fusion.69
  41.2 0.7 fusion.71
  41.9 5.8 %fusion.6 = (f32[8,512]{1,0:T(8,128)S(1)}, f32[8,512,512]{1,2,0:T(8,128)}) fusion(f32[8,512]{1,0:T(8,128)S(1)} %add_bitcast_fusion.1, pred[512,512]{0,1:T(8,128)(4,1)S(1)} %iota_compare_fusion.1, bf16[512,8,273]{0,2,1:T(8,128)(2,1)S(1)} %get-tuple-element.192, bf16[512,8,273]{0,2,1:T(8,128)(2,1)S(1)} %copy-done.4), kind=kOutput, calls=%fused_computation.14 | convolution fusion | flops 1153429504 | bytes 13156352 | tf_op jit(solution)/shard_map/sjz,djz->jsd/dot_general | solution.py:99
  47.7 17.2 %all-gather.2 = f32[8,1,8]{2,1,0:T(1,128)S(1)} all-gather(f32[1,1,8]{2,1,0:T(1,128)S(1)} %bitcast.169), channel_id=1, replica_groups=mesh['grp'=2,'seq'=8,'head'=2] {'seq'}, dimensions={0}, use_global_device_ids=true | all-gather | bytes 288 | tf_op jit(solution)/shard_map/all_gather | solution.py:18
  64.9 31.3 %all-gather.1 = f32[64,273]{1,0:T(8,128)S(1)} all-gather(f32[8,273]{1,0:T(8,128)S(1)} %fusion.73), channel_id=3, replica_groups=mesh['grp'=2,'seq'=8,'head'=2] {'seq'}, dimensions={0}, use_global_device_ids=true | all-gather | bytes 78624 | tf_op jit(solution)/shard_map/all_gather | solution.py:18
  96.3 2.7 %fusion.38 = f32[8,576,512]{2,1,0:T(8,128)S(1)} fusion(bf16[512,1024]{1,0:T(8,128)(2,1)} %param.13, bf16[64,1024]{1,0:T(8,128)(2,1)} %collective-permute-done.1, bf16[512,1024]{1,0:T(8,128)(2,1)S(1)} %copy-done), kind=kOutput, calls=%fused_computation.45 | convolution fusion | flops 606339072 | bytes 11665408 | tf_op jit(solution)/shard_map/qhd,khd->hqk/dot_general | solution.py:122
  99.0 6.7 %fusion.91 = (f32[8,512]{1,0:T(8,128)S(1)}, f32[8,512,576]{1,2,0:T(8,128)}) fusion(f32[8,576,512]{2,1,0:T(8,128)S(1)} %fusion.38, pred[512,576]{0,1:T(8,128)(4,1)S(1)} %copy-done.10), kind=kOutput, calls=%fused_computation.127 | output fusion | flops 14156351 | bytes 19185664 | tf_op jit(solution)/shard_map/sub | solution.py:134
  105.7 6.2 %fusion.10 = f32[8,128,512]{2,1,0:T(8,128)} fusion(f32[8,512,576]{1,2,0:T(8,128)} %get-tuple-element.194, f32[8,512]{1,0:T(8,128)S(1)} %get-tuple-element.193, bf16[576,1024]{1,0:T(8,128)(2,1)S(1)} %copy-done.7), kind=kOutput, calls=%fused_computation.18 | convolution fusion | flops 608698368 | bytes 12730368 | tf_op jit(solution)/shard_map/hqk,khd->qhd/dot_general | solution.py:137
  111.9 52.6 %all-gather.5.cloned.1.call-done = f32[64,273,128]{2,0,1:T(8,128)} async-done(((f32[8,273,128]{2,0,1:T(8,128)}), f32[64,273,128]{2,0,1:T(8,128)}) %all-gather.5.cloned.1.call-update) | async-done | bytes 8945680 | tf_op jit(solution)/shard_map/all_gather | solution.py:18
  164.5 37.3 %while.16 = (s32[]{:T(128)}, f32[8,273,128]{2,1,0:T(8,128)}, f32[8,273]{1,0:T(8,128)S(1)}, s32[]{:T(128)}, f32[8,8]{1,0:T(8,128)S(1)}, /*index=5*/f32[8,8,273,12...) while((s32[]{:T(128)}, f32[8,273,128]{2,1,0:T(8,128)}, f32[8,273]{1,0:T(8,128)S(1)}, ...), condition=%wide.region_3.4_spmd.clone, body=%wide.region_2.3_spmd.clone.sunk | while | flops 1126948 | bytes 5617511 | solution.py:27
  164.5 2.3 %constant_dynamic-slice_fusion.3 = f32[1,8,273,128]{3,1,0,2:T(8,128)} fusion(f32[8,8,273,128]{3,1,0,2:T(8,128)} %get-tuple-element.265, s32[]{:T(128)S(6)} %copy.124), kind=kLoop, calls=%fused_computation.5.clone.1 | loop fusion | bytes 2236420 | tf_op jit(solution)/shard_map/while/body/eval_jaxpr/dynamic_slice | solution.py:24
  166.8 2.6 %fusion.112 = f32[8,273,128]{2,1,0:T(8,128)} fusion(f32[1,8,273,128]{3,1,0,2:T(8,128)} %constant_dynamic-slice_fusion.3, f32[8,273,128]{2,1,0:T(8,128)} %get-tuple-element.252, f32[8]{0:T(128)S(1)} %fusion.111, pred[]{:T(512)S(6)} %compare.3, pred[]{:T(512)S(6)} %lt.24), kind=kLoop, calls=%fused_computation.2.clone.1 | loop fusion | flops 1118208 | bytes 3354658 | tf_op jit(solution)/shard_map/while/body/eval_jaxpr/jit(_where)/select_n | solution.py:25
  169.4 0.1 fusion.113
  169.5 2.3 %constant_dynamic-slice_fusion.3 = f32[1,8,273,128]{3,1,0,2:T(8,128)} fusion(f32[8,8,273,128]{3,1,0,2:T(8,128)} %get-tuple-element.265, s32[]{:T(128)S(6)} %copy.124), kind=kLoop, calls=%fused_computation.5.clone.1 | loop fusion | bytes 2236420 | tf_op jit(solution)/shard_map/while/body/eval_jaxpr/dynamic_slice | solution.py:24
  171.8 3.0 %fusion.112 = f32[8,273,128]{2,1,0:T(8,128)} fusion(f32[1,8,273,128]{3,1,0,2:T(8,128)} %constant_dynamic-slice_fusion.3, f32[8,273,128]{2,1,0:T(8,128)} %get-tuple-element.252, f32[8]{0:T(128)S(1)} %fusion.111, pred[]{:T(512)S(6)} %compare.3, pred[]{:T(512)S(6)} %lt.24), kind=kLoop, calls=%fused_computation.2.clone.1 | loop fusion | flops 1118208 | bytes 3354658 | tf_op jit(solution)/shard_map/while/body/eval_jaxpr/jit(_where)/select_n | solution.py:25
  174.8 0.1 fusion.113
  174.9 2.3 %constant_dynamic-slice_fusion.3 = f32[1,8,273,128]{3,1,0,2:T(8,128)} fusion(f32[8,8,273,128]{3,1,0,2:T(8,128)} %get-tuple-element.265, s32[]{:T(128)S(6)} %copy.124), kind=kLoop, calls=%fused_computation.5.clone.1 | loop fusion | bytes 2236420 | tf_op jit(solution)/shard_map/while/body/eval_jaxpr/dynamic_slice | solution.py:24
  177.2 3.0 %fusion.112 = f32[8,273,128]{2,1,0:T(8,128)} fusion(f32[1,8,273,128]{3,1,0,2:T(8,128)} %constant_dynamic-slice_fusion.3, f32[8,273,128]{2,1,0:T(8,128)} %get-tuple-element.252, f32[8]{0:T(128)S(1)} %fusion.111, pred[]{:T(512)S(6)} %compare.3, pred[]{:T(512)S(6)} %lt.24), kind=kLoop, calls=%fused_computation.2.clone.1 | loop fusion | flops 1118208 | bytes 3354658 | tf_op jit(solution)/shard_map/while/body/eval_jaxpr/jit(_where)/select_n | solution.py:25
  180.2 0.1 fusion.113
  180.3 2.3 %constant_dynamic-slice_fusion.3 = f32[1,8,273,128]{3,1,0,2:T(8,128)} fusion(f32[8,8,273,128]{3,1,0,2:T(8,128)} %get-tuple-element.265, s32[]{:T(128)S(6)} %copy.124), kind=kLoop, calls=%fused_computation.5.clone.1 | loop fusion | bytes 2236420 | tf_op jit(solution)/shard_map/while/body/eval_jaxpr/dynamic_slice | solution.py:24
  182.6 3.0 %fusion.112 = f32[8,273,128]{2,1,0:T(8,128)} fusion(f32[1,8,273,128]{3,1,0,2:T(8,128)} %constant_dynamic-slice_fusion.3, f32[8,273,128]{2,1,0:T(8,128)} %get-tuple-element.252, f32[8]{0:T(128)S(1)} %fusion.111, pred[]{:T(512)S(6)} %compare.3, pred[]{:T(512)S(6)} %lt.24), kind=kLoop, calls=%fused_computation.2.clone.1 | loop fusion | flops 1118208 | bytes 3354658 | tf_op jit(solution)/shard_map/while/body/eval_jaxpr/jit(_where)/select_n | solution.py:25
  185.6 2.3 %constant_dynamic-slice_fusion.3 = f32[1,8,273,128]{3,1,0,2:T(8,128)} fusion(f32[8,8,273,128]{3,1,0,2:T(8,128)} %get-tuple-element.265, s32[]{:T(128)S(6)} %copy.124), kind=kLoop, calls=%fused_computation.5.clone.1 | loop fusion | bytes 2236420 | tf_op jit(solution)/shard_map/while/body/eval_jaxpr/dynamic_slice | solution.py:24
  188.0 3.0 %fusion.112 = f32[8,273,128]{2,1,0:T(8,128)} fusion(f32[1,8,273,128]{3,1,0,2:T(8,128)} %constant_dynamic-slice_fusion.3, f32[8,273,128]{2,1,0:T(8,128)} %get-tuple-element.252, f32[8]{0:T(128)S(1)} %fusion.111, pred[]{:T(512)S(6)} %compare.3, pred[]{:T(512)S(6)} %lt.24), kind=kLoop, calls=%fused_computation.2.clone.1 | loop fusion | flops 1118208 | bytes 3354658 | tf_op jit(solution)/shard_map/while/body/eval_jaxpr/jit(_where)/select_n | solution.py:25
  191.0 2.3 %constant_dynamic-slice_fusion.3 = f32[1,8,273,128]{3,1,0,2:T(8,128)} fusion(f32[8,8,273,128]{3,1,0,2:T(8,128)} %get-tuple-element.265, s32[]{:T(128)S(6)} %copy.124), kind=kLoop, calls=%fused_computation.5.clone.1 | loop fusion | bytes 2236420 | tf_op jit(solution)/shard_map/while/body/eval_jaxpr/dynamic_slice | solution.py:24
  193.3 3.0 %fusion.112 = f32[8,273,128]{2,1,0:T(8,128)} fusion(f32[1,8,273,128]{3,1,0,2:T(8,128)} %constant_dynamic-slice_fusion.3, f32[8,273,128]{2,1,0:T(8,128)} %get-tuple-element.252, f32[8]{0:T(128)S(1)} %fusion.111, pred[]{:T(512)S(6)} %compare.3, pred[]{:T(512)S(6)} %lt.24), kind=kLoop, calls=%fused_computation.2.clone.1 | loop fusion | flops 1118208 | bytes 3354658 | tf_op jit(solution)/shard_map/while/body/eval_jaxpr/jit(_where)/select_n | solution.py:25
  196.3 0.1 fusion.113
  196.4 2.3 %constant_dynamic-slice_fusion.3 = f32[1,8,273,128]{3,1,0,2:T(8,128)} fusion(f32[8,8,273,128]{3,1,0,2:T(8,128)} %get-tuple-element.265, s32[]{:T(128)S(6)} %copy.124), kind=kLoop, calls=%fused_computation.5.clone.1 | loop fusion | bytes 2236420 | tf_op jit(solution)/shard_map/while/body/eval_jaxpr/dynamic_slice | solution.py:24
  198.7 3.0 %fusion.112 = f32[8,273,128]{2,1,0:T(8,128)} fusion(f32[1,8,273,128]{3,1,0,2:T(8,128)} %constant_dynamic-slice_fusion.3, f32[8,273,128]{2,1,0:T(8,128)} %get-tuple-element.252, f32[8]{0:T(128)S(1)} %fusion.111, pred[]{:T(512)S(6)} %compare.3, pred[]{:T(512)S(6)} %lt.24), kind=kLoop, calls=%fused_computation.2.clone.1 | loop fusion | flops 1118208 | bytes 3354658 | tf_op jit(solution)/shard_map/while/body/eval_jaxpr/jit(_where)/select_n | solution.py:25
  201.8 2.5 %fusion.65 = f32[8,128,512]{2,1,0:T(8,128)S(1)} fusion(bf16[512,8,273]{0,2,1:T(8,128)(2,1)S(1)} %get-tuple-element.192, f32[8,273,128]{2,1,0:T(8,128)} %get-tuple-element.130), kind=kOutput, calls=%fused_computation.76 | convolution fusion | flops 288218112 | bytes 5451776 | tf_op jit(solution)/shard_map/thf,hfd->thd/dot_general | solution.py:53
  204.3 0.8 fusion.57
  205.1 0.8 fusion.59
  205.9 0.4 fusion.74
  206.4 0.4 fusion.76
  206.8 0.4 fusion.78
  207.3 0.7 slice-done.1
  208.0 0.2 copy-done.9
  208.2 0.8 copy-done.18
  208.9 3.1 %fusion.18 = bf16[512,8,128]{0,2,1:T(8,128)(2,1)S(1)} fusion(f32[8,128,512]{2,1,0:T(8,128)S(1)} %copy-done.18, f32[8,128,512]{2,1,0:T(8,128)S(1)} %fusion.65, f32[8,128,512]{2,1,0:T(8,128)S(1)} %fusion.57, f32[8,128,512]{2,1,0:T(8,128)S(1)} %fusion.59, f32[8,512,512]{1,2,0:T(8,128)S(1)} %bitcast.171, f32[8,512]{1,0:T(8,128)S(1)} %copy-done.16, ...), kind=kOutput, calls=%fused_computation.30 | convolution fusion | flops 548929536 | bytes 19185664 | tf_op jit(solution)/shard_map/hqk,khd->qhd/dot_general | solution.py:103
  212.1 1.3 copy.48
  (69 shorter events, 0.6 us)
Async XLA Ops:
  6.5 89.7 %copy-start = (bf16[512,1024]{1,0:T(8,128)(2,1)S(1)}, bf16[512,1024]{1,0:T(8,128)(2,1)}, u32[]{:S(2)}) copy-start(bf16[512,1024]{1,0:T(8,128)(2,1)} %param.12) | copy-start | bytes 3145732
  6.5 10.2 %copy-start.13 = (bf16[512,128]{1,0:T(8,128)(2,1)S(1)}, bf16[512,128]{1,0:T(8,128)(2,1)}, u32[]{:S(2)}) copy-start(bf16[512,128]{1,0:T(8,128)(2,1)} %param.9) | copy-start | bytes 393220
  6.5 157.9 %all-gather.5.cloned.1.call-start = ((), (), s32[]{:S(2)}) async-start(), calls=%async_computation | async-start | bytes 10063872 | tf_op jit(solution)/shard_map/all_gather | solution.py:18
  8.2 16.4 %collective-permute-start = (bf16[64,1024]{1,0:T(8,128)(2,1)}, bf16[64,1024]{1,0:T(8,128)(2,1)}, u32[]{:S(2)}, u32[]{:S(2)}) collective-permute-start(bf16[64,1024]{1,0:T(8,128)(2,1)} %slice.32), channel_id=1, source_target_pairs={{0,2},{2,4},{4,6},{6,8},{8,10},{10,12},{12,14},{1,3},{3,5},{5,7},{... | collective-permute-start | bytes 393224 | tf_op jit(solution)/shard_map/ppermute | solution.py:13
  16.7 2.8 %copy-start.14 = (f32[512,8]{0,1:T(8,128)S(1)}, f32[512,8]{0,1:T(8,128)}, u32[]{:S(2)}) copy-start(f32[512,8]{0,1:T(8,128)} %param.14) | copy-start | bytes 49156
  16.7 4.5 %copy-start.17 = (f32[3,1024]{1,0:T(4,128)S(1)}, f32[3,1024]{1,0:T(4,128)}, u32[]{:S(2)}) copy-start(f32[3,1024]{1,0:T(4,128)} %param.15) | copy-start | bytes 36868
  21.2 4.4 %copy-start.5 = (bf16[512,1024]{1,0:T(8,128)(2,1)S(1)}, bf16[512,1024]{1,0:T(8,128)(2,1)}, u32[]{:S(2)}) copy-start(bf16[512,1024]{1,0:T(8,128)(2,1)} %param.11) | copy-start | bytes 3145732
  24.5 4.5 %copy-start.3 = (bf16[512,8,273]{0,2,1:T(8,128)(2,1)}, bf16[512,8,273]{0,2,1:T(8,128)(2,1)S(1)}, u32[]{:S(2)}) copy-start(bf16[512,8,273]{0,2,1:T(8,128)(2,1)S(1)} %get-tuple-element.191) | copy-start | bytes 6709252
  25.7 2.1 copy-start.6
  26.6 2.5 %copy-start.8 = (bf16[64,8,8,128]{3,2,1,0:T(8,128)(2,1)}, bf16[64,8,8,128]{3,2,1,0:T(8,128)(2,1)S(1)}, u32[]{:S(2)}) copy-start(bf16[64,8,8,128]{3,2,1,0:T(8,128)(2,1)S(1)} %fusion.45) | copy-start | bytes 3145732
  33.1 63.1 %collective-permute-start.1 = (bf16[64,1024]{1,0:T(8,128)(2,1)}, bf16[64,1024]{1,0:T(8,128)(2,1)}, u32[]{:S(2)}, u32[]{:S(2)}) collective-permute-start(bf16[64,1024]{1,0:T(8,128)(2,1)} %slice.39), channel_id=1, source_target_pairs={{0,2},{2,4},{4,6},{6,8},{8,10},{10,12},{12,14},{1,3},{3,5},{5,7},{... | collective-permute-start | bytes 393224 | tf_op jit(solution)/shard_map/ppermute | solution.py:13
  36.6 3.9 %copy-start.4 = (bf16[512,8,273]{0,2,1:T(8,128)(2,1)S(1)}, bf16[512,8,273]{0,2,1:T(8,128)(2,1)}, u32[]{:S(2)}) copy-start(bf16[512,8,273]{0,2,1:T(8,128)(2,1)} %copy-done.3) | copy-start | bytes 6709252
  36.7 5.2 %copy-start.11 = (pred[512,512]{0,1:T(8,128)(4,1)}, pred[512,512]{0,1:T(8,128)(4,1)S(1)}, u32[]{:S(2)}) copy-start(pred[512,512]{0,1:T(8,128)(4,1)S(1)} %iota_compare_fusion.1) | copy-start | bytes 786436
  36.8 5.1 %copy-start.15 = (f32[8,512]{1,0:T(8,128)}, f32[8,512]{1,0:T(8,128)S(1)}, u32[]{:S(2)}) copy-start(f32[8,512]{1,0:T(8,128)S(1)} %add_bitcast_fusion.1) | copy-start | bytes 49156
  96.2 2.7 %copy-start.10 = (pred[512,576]{0,1:T(8,128)(4,1)S(1)}, pred[512,576]{0,1:T(8,128)(4,1)}, u32[]{:S(2)}) copy-start(pred[512,576]{0,1:T(8,128)(4,1)} %fusion.44) | copy-start | bytes 884740
  99.0 6.7 %copy-start.7 = (bf16[576,1024]{1,0:T(8,128)(2,1)S(1)}, bf16[576,1024]{1,0:T(8,128)(2,1)}, u32[]{:S(2)}) copy-start(bf16[576,1024]{1,0:T(8,128)(2,1)} %copy-done.6) | copy-start | bytes 3538948
  201.8 2.5 %copy-start.2 = (f32[8,273,128]{2,1,0:T(8,128)S(1)}, f32[8,273,128]{2,1,0:T(8,128)}, u32[]{:S(2)}) copy-start(f32[8,273,128]{2,1,0:T(8,128)} %get-tuple-element.130) | copy-start | bytes 3354628
  204.3 2.9 %slice-start = ((s8[8388608]{0:T(1024)(128)(4,1)}), s8[4194304]{0:T(1024)(128)(4,1)S(1)}, s32[]{:S(2)}) async-start(s8[8388608]{0:T(1024)(128)(4,1)} %bitcast.170), calls=%async_computation.1 | async-start | bytes 8388608
  205.1 2.9 %slice-start.1 = ((s8[8388608]{0:T(1024)(128)(4,1)}), s8[4194304]{0:T(1024)(128)(4,1)S(1)}, s32[]{:S(2)}) async-start(s8[8388608]{0:T(1024)(128)(4,1)} %bitcast.170), calls=%async_computation.2 | async-start | bytes 8388608
  206.4 1.8 copy-start.9
  206.4 1.8 copy-start.12
  206.4 1.8 copy-start.16
  206.4 2.6 %copy-start.18 = (f32[8,128,512]{2,1,0:T(8,128)S(1)}, f32[8,128,512]{2,1,0:T(8,128)}, u32[]{:S(2)}) copy-start(f32[8,128,512]{2,1,0:T(8,128)} %fusion.10) | copy-start | bytes 6291460
  208.9 4.4 %copy-start.1 = (bf16[512,1024]{1,0:T(8,128)(2,1)S(1)}, bf16[512,1024]{1,0:T(8,128)(2,1)}, u32[]{:S(2)}) copy-start(bf16[512,1024]{1,0:T(8,128)(2,1)} %param.12) | copy-start | bytes 3145732
Sparse Core Ops, SparseCore 0:
  31.7 132.6 all-gather.4
where the time goes:
time: 221 us; the launch traced here: 220 us
  waiting for transfers between devices  52.6 us (24%)
  blocking collectives  48.5 us (22%)
  other arithmetic  39.2 us (18%)
  matrix products  30.8 us (14%)
  local copies, waits for them, and re-layouts  26.4 us (12%)
  between operations  13.7 us (6%)
  starting transfers between devices  8.95 us (4%)
    all_gather x1, waiting for transfers between devices, prefix(): pieces = jax.tree.map(lambda part: lax.all_gather(part, axis), value)  52.6 us
    all_gather x2, blocking collectives, prefix(): pieces = jax.tree.map(lambda part: lax.all_gather(part, axis), value)  48.5 us
    select_n x14, other arithmetic, hop(): jnp.where(position < mine, new, old)  21.1 us
    dynamic_slice x7, local copies, waits for them, and re-layouts, hop(): longer = join(so_far, jax.tree.map(lambda part: part[position], pieces))  16.2 us
    dot_general x12, matrix products, divided_product(): term = jnp.einsum(form, narrow, piece, preferred_element_type=jnp.float32)  13.1 us
    ppermute x2, starting transfers between devices, passed_along(): return lax.ppermute(block, axis, route)  8.95 us
    sub x1, other arithmetic, local(): weights = jnp.exp(win_scores - top)  6.71 us
    dot_general x1, matrix products, local(): jnp.einsum('hqk,khd->qhd', probs, win_values, preferred_element_type=jnp....  6.18 us
  transfers between devices with their start and end apart: 3, of which 1 were waited for; matrix products, arithmetic and copies ran while one was open for 18% of the time, Pallas kernels for 0%

commit v1 on v0

v1 whole, which is shorter than its diff:
```python
import functools

import jax
import jax.numpy as jnp
from jax import lax
from jax.experimental import pallas as pl
from jax.experimental.pallas import tpu as pltpu
from jax.sharding import PartitionSpec as P

WINDOW = 64
TILE = 128
FOLDED = 160
F32 = jnp.float32
BF16 = jnp.bfloat16
MESH = pl.DeviceIdType.MESH


def dot(a, b):
    return lax.dot_general(a, b, (((1,), (0,)), ((), ())), preferred_element_type=F32)


def dot_t(a, b):
    return lax.dot_general(a, b, (((1,), (1,)), ((), ())), preferred_element_type=F32)


def dot_first(a, b):
    return lax.dot_general(a, b, (((0,), (0,)), ((), ())), preferred_element_type=F32)


def fold_features(x, square_scale, pair_scale, linear_scale):
    rows = lax.broadcasted_iota(jnp.int32, x.shape, 0)
    scaled = x * pair_scale
    parts = [(x * square_scale) * x]
    for step in range(1, 8):
        parts.append(scaled * pltpu.roll(x, 16 - step, 0))
    half = scaled * pltpu.roll(x, 8, 0)
    parts.append(jnp.where(rows < 8, half, jnp.where(rows == 8, 1.0, 0.0)))
    parts.append(x * linear_scale)
    return jnp.concatenate([part.astype(BF16) for part in parts], axis=0)


def kernel(
    n, heads, size, width,
    qf, kf, gates, weight, values, win_key, win_query,
    out,
    vx, kx, wq, halo, vf, vw, qt, kt, phiq, numden, win, ccol, crow,
    s_send, s_recv, side, e_send, e_recv,
    in_sem, halo_send, halo_recv, ss_sem, sr_sem, ds_sem, dr_sem, es_sem, er_sem,
):
    me = lax.axis_index("seq")
    tok = qf.shape[0]
    per_head = n // heads
    rows = FOLDED // per_head
    tiles = tok // TILE
    tail = WINDOW

    load_v = pltpu.make_async_copy(values, vx.at[pl.ds(tail, tok)], in_sem.at[0])
    load_k = pltpu.make_async_copy(win_key, kx.at[pl.ds(tail, tok)], in_sem.at[1])
    load_q = pltpu.make_async_copy(win_query, wq, in_sem.at[2])
    load_v.start()
    load_k.start()
    load_q.start()

    barrier = pltpu.get_barrier_semaphore()
    for peer in range(n):
        @pl.when(peer != me)
        def _(peer=peer):
            pl.semaphore_signal(barrier, inc=1, device_id={"seq": peer}, device_id_type=MESH)

    @pl.when(me == 0)
    def _():
        vx[0:tail, :] = jnp.zeros((tail, heads * size), BF16)
        kx[0:tail, :] = jnp.zeros((tail, heads * size), BF16)
        halo[...] = jnp.zeros(halo.shape, BF16)

    pl.semaphore_wait(barrier, n - 1)

    nxt = lax.rem(me + 1, n)

    def halo_copies():
        short = pltpu.make_async_remote_copy(
            values.at[pl.ds(tok - 16, 16)], halo, halo_send.at[0], halo_recv.at[0],
            device_id={"seq": nxt}, device_id_type=MESH)
        long_v = pltpu.make_async_remote_copy(
            values.at[pl.ds(tok - tail, tail)], vx.at[pl.ds(0, tail)], halo_send.at[1], halo_recv.at[1],
            device_id={"seq": nxt}, device_id_type=MESH)
        long_k = pltpu.make_async_remote_copy(
            win_key.at[pl.ds(tok - tail, tail)], kx.at[pl.ds(0, tail)], halo_send.at[2], halo_recv.at[2],
            device_id={"seq": nxt}, device_id_type=MESH)
        return short, long_v, long_k

    @pl.when(me < n - 1)
    def _():
        for copy in halo_copies():
            copy.start()

    def s_copy(block):
        return pltpu.make_async_remote_copy(
            s_send.at[block], s_recv.at[me], ss_sem.at[block], sr_sem.at[me],
            device_id={"seq": block}, device_id_type=MESH)

    def s_arrival(source):
        return pltpu.make_async_remote_copy(
            s_send.at[source], s_recv.at[source], ss_sem.at[source], sr_sem.at[source],
            device_id={"seq": source}, device_id_type=MESH)

    def d_copy(peer):
        return pltpu.make_async_remote_copy(
            side.at[me], side.at[me], ds_sem.at[peer], dr_sem.at[me],
            device_id={"seq": peer}, device_id_type=MESH)

    def d_arrival(source):
        return pltpu.make_async_remote_copy(
            side.at[source], side.at[source], ds_sem.at[source], dr_sem.at[source],
            device_id={"seq": source}, device_id_type=MESH)

    def e_copy(peer):
        return pltpu.make_async_remote_copy(
            e_send.at[peer], e_recv.at[me], es_sem.at[peer], er_sem.at[me],
            device_id={"seq": peer}, device_id_type=MESH)

    def e_arrival(source):
        return pltpu.make_async_remote_copy(
            e_send.at[source], e_recv.at[source], es_sem.at[source], er_sem.at[source],
            device_id={"seq": source}, device_id_type=MESH)

    lower = jnp.where(
        lax.broadcasted_iota(jnp.int32, (tok, tok), 0) >= lax.broadcasted_iota(jnp.int32, (tok, tok), 1),
        1.0, 0.0).astype(BF16)
    wide = jnp.concatenate([gates[...], jnp.zeros((tok, 128 - heads), F32)], axis=1)
    upper = wide.astype(BF16)
    rest = wide - upper.astype(F32)
    middle = rest.astype(BF16)
    lowest = (rest - middle.astype(F32)).astype(BF16)
    total = dot(lower, upper) + (dot(lower, middle) + dot(lower, lowest))
    ccol[...] = total
    turned = total.T
    crow[...] = turned[0:heads, :]
    kt[...] = kf[...].astype(F32).T
    qt[...] = qf[...].astype(F32).T
    keep_row = jnp.exp(crow[:, tok - 1:tok] - crow[...])
    keep_hi = keep_row.astype(BF16)
    keep_lo = (keep_row - keep_hi.astype(F32)).astype(BF16)
    finish = jnp.exp(crow[:, tok - 1:tok])

    load_v.wait()

    @pl.when(me > 0)
    def _():
        halo_copies()[0].wait_recv()

    head_row = lax.broadcasted_iota(jnp.int32, (heads, FOLDED), 0)
    norm = jnp.zeros((heads, FOLDED), F32)
    for h in range(heads):
        lanes = slice(h * size, (h + 1) * size)
        phik = fold_features(kt[h * width:(h + 1) * width, :], 1.0, 1.0, 1.0)
        current = vx[tail:tail + tok, lanes].astype(F32)
        vf[8:8 + tok, :] = current
        vf[0:8, :] = halo[:, lanes].astype(F32)[8:16, :]
        conv = weight[0:1, lanes] * current
        for tap in range(1, weight.shape[0]):
            conv = conv + weight[tap:tap + 1, lanes] * vf[8 - tap:8 - tap + tok, :]
        conv = conv.astype(BF16)
        vw[h, :, 0:size] = conv
        vw[h, :, size:2 * size] = jnp.ones((tok, size), BF16)
        column = ccol[:, h:h + 1]
        keep = jnp.exp(ccol[tok - 1:tok, h:h + 1] - column)
        state = dot(phik, (conv.astype(F32) * keep).astype(BF16))
        norm_h = dot_t(keep_hi, phik) + dot_t(keep_lo, phik)
        norm = jnp.where(head_row == h, norm_h, norm)
        for b in range(per_head):
            block = h * per_head + b
            piece = state[b * rows:(b + 1) * rows, :].astype(BF16)

            @pl.when(block != me)
            def _(block=block, piece=piece):
                s_send[block] = piece
                s_copy(block).start()

            @pl.when(block == me)
            def _(piece=piece):
                s_recv[me] = piece

    side[me] = jnp.concatenate([norm, jnp.broadcast_to(finish, (heads, 256 - FOLDED))], axis=1)
    for peer in range(n):
        @pl.when(peer != me)
        def _(peer=peer):
            d_copy(peer).start()

    lane_head = lax.broadcasted_iota(jnp.int32, (tok, heads * width), 1) // width
    kt_narrow = kt[...].astype(BF16)
    q_quarter = qf[...] * jnp.asarray(0.25, BF16)
    diagonal = (lax.broadcasted_iota(jnp.int32, (TILE, TILE), 0)
                >= lax.broadcasted_iota(jnp.int32, (TILE, TILE), 1))
    for h in range(heads):
        lone = jnp.where(lane_head == h, q_quarter, jnp.zeros_like(q_quarter))
        for i in range(tiles):
            t0 = i * TILE
            reach = t0 + TILE
            x = dot(lone[t0:reach, :], kt_narrow[:, 0:reach])
            poly = 1.0 + x * (1.0 + 0.5 * x)
            gap = ccol[t0:reach, h:h + 1] - crow[h:h + 1, 0:reach]
            last = jnp.where(diagonal, gap[:, t0:reach], -1e30)
            if i > 0:
                gap = jnp.concatenate([gap[:, 0:t0], last], axis=1)
            else:
                gap = last
            score = (poly * jnp.exp(gap)).astype(BF16)
            numden[h, t0:reach, :] = dot(score, vw[h, 0:reach, :])

    for source in range(n):
        @pl.when(source != me)
        def _(source=source):
            s_arrival(source).wait_recv()
            d_arrival(source).wait_recv()

    mine = me // per_head
    running = jnp.zeros((rows, size), F32)
    for i in range(n):
        narrow = running.astype(BF16)

        @pl.when(i != me)
        def _(i=i, narrow=narrow):
            e_send[i] = narrow
            e_copy(i).start()

        @pl.when(i == me)
        def _(narrow=narrow):
            e_recv[me] = narrow

        fade = side[i, pl.ds(mine, 1), :][:, 192:193]
        running = fade * running + s_recv[i].astype(F32)

    norm_before = jnp.zeros((heads, 256), F32)
    for i in range(n):
        block = side[i]
        joined = block[:, 192:193] * norm_before + block
        norm_before = jnp.where(i < me, joined, norm_before)
    norm_col = jnp.concatenate([norm_before, jnp.zeros((128 - heads, 256), F32)], axis=0).T

    load_k.wait()
    load_q.wait()

    @pl.when(me > 0)
    def _():
        halo_copies()[1].wait_recv()
        halo_copies()[2].wait_recv()

    r = lax.broadcasted_iota(jnp.int32, (WINDOW, 2 * WINDOW), 0)
    j = lax.broadcasted_iota(jnp.int32, (WINDOW, 2 * WINDOW), 1)
    band = (j > r) & (j <= r + WINDOW)
    first = band & ((j >= WINDOW) | (me > 0))
    scale = size ** (-0.5)
    ones = jnp.ones((2 * WINDOW, size), BF16)
    for h in range(heads):
        lanes = slice(h * size, (h + 1) * size)
        for i in range(tok // WINDOW):
            t0 = i * WINDOW
            s = dot_t(wq[t0:t0 + WINDOW, lanes], kx[t0:t0 + 2 * WINDOW, lanes]) * scale
            s = jnp.where(first if i == 0 else band, s, -1e30)
            p = jnp.exp(s - jnp.max(s, axis=1, keepdims=True)).astype(BF16)
            pv = dot(p, jnp.concatenate([vx[t0:t0 + 2 * WINDOW, lanes], ones], axis=1))
            win[t0:t0 + WINDOW, lanes] = pv[:, 0:size] / pv[:, size:2 * size]

    for h in range(heads):
        phiq[h] = fold_features(qt[h * width:(h + 1) * width, :], 1.0 / 32, 1.0 / 16, 0.25)

    for source in range(n):
        @pl.when(source != me)
        def _(source=source):
            e_arrival(source).wait_recv()

    for h in range(heads):
        lanes = slice(h * size, (h + 1) * size)
        before = jnp.concatenate([e_recv[h * per_head + b] for b in range(per_head)], axis=0)
        norm_wide = jnp.broadcast_to(norm_col[0:FOLDED, h:h + 1], (FOLDED, size)).astype(BF16)
        both = dot_first(phiq[h], jnp.concatenate([before, norm_wide], axis=1))
        both = numden[h] + jnp.exp(ccol[:, h:h + 1]) * both
        out[:, lanes] = (both[:, 0:size] / both[:, size:2 * size] + win[:, lanes]).astype(BF16)

    @pl.when(me < n - 1)
    def _():
        for copy in halo_copies():
            copy.wait_send()

    for peer in range(n):
        @pl.when(peer != me)
        def _(peer=peer):
            s_copy(peer).wait_send()
            d_copy(peer).wait_send()
            e_copy(peer).wait_send()


def solution(mesh):
    n = mesh.shape["seq"]

    def local(q_feat, k_feat, values, win_query, win_key, log_gates, conv_weight):
        tok, channels = values.shape
        heads = log_gates.shape[1]
        size = channels // heads
        width = q_feat.shape[1] // heads
        rows = FOLDED * heads // n
        vmem = pl.BlockSpec(memory_space=pltpu.VMEM)
        anywhere = pl.BlockSpec(memory_space=pl.ANY)
        dma = pltpu.SemaphoreType.DMA
        return pl.pallas_call(
            functools.partial(kernel, n, heads, size, width),
            out_shape=jax.ShapeDtypeStruct((tok, channels), BF16),
            in_specs=[vmem] * 4 + [anywhere] * 3,
            out_specs=vmem,
            scratch_shapes=[
                pltpu.VMEM((tok + WINDOW, channels), BF16),
                pltpu.VMEM((tok + WINDOW, channels), BF16),
                pltpu.VMEM((tok, channels), BF16),
                pltpu.VMEM((16, channels), BF16),
                pltpu.VMEM((tok + 8, size), F32),
                pltpu.VMEM((heads, tok, 2 * size), BF16),
                pltpu.VMEM((heads * width, tok), F32),
                pltpu.VMEM((heads * width, tok), F32),
                pltpu.VMEM((heads, FOLDED, tok), BF16),
                pltpu.VMEM((heads, tok, 2 * size), F32),
                pltpu.VMEM((tok, channels), F32),
                pltpu.VMEM((tok, 128), F32),
                pltpu.VMEM((heads, tok), F32),
                pltpu.VMEM((n, rows, size), BF16),
                pltpu.VMEM((n, rows, size), BF16),
                pltpu.VMEM((n, heads, 256), F32),
                pltpu.VMEM((n, rows, size), BF16),
                pltpu.VMEM((n, rows, size), BF16),
                dma((3,)), dma((3,)), dma((3,)),
                dma((n,)), dma((n,)), dma((n,)), dma((n,)), dma((n,)), dma((n,)),
            ],
            compiler_params=pltpu.CompilerParams(
                collective_id=0, has_side_effects=True, vmem_limit_bytes=48 * 1024 * 1024),
        )(q_feat, k_feat, log_gates, conv_weight, values, win_key, win_query)

    shard = P(("grp", "seq"), "head")
    return jax.shard_map(
        local, mesh=mesh, in_specs=(shard,) * 6 + (P(None, "head"),), out_specs=shard, check_vma=False)
```

time: 221 us -> 48.2 us (0.22)
  the two profiles are of different devices: /device:TPU:0 before, /device:TPU:24 now
where the time goes in v1:
time: 48.2 us; the launch traced here: 48 us
  Pallas kernels  42.3 us (88%)
  local copies, waits for them, and re-layouts  5.62 us (12%)
    pallas_call x1, Pallas kernels, local(): pl.pallas_call(functools.partial(kernel, n, heads, size, width), out_shap...  42.3 us
    unnamed x14, local copies, waits for them, and re-layouts  5.62 us

profile of v1, /device:TPU:24, one launch (start us, length us, event | category | flops | bytes accessed | tf_op | source)
XLA Modules:
  0.0 48.0 jit_solution(4840592324746836835)
XLA Ops:
  0.0 0.0 copy-start.5
  0.0 0.0 copy-start.4
  0.0 0.0 copy-start.3
  0.0 0.9 %copy.8.gates = f32[512,8]{1,0:T(8,128)S(1)} copy(f32[512,8]{0,1:T(8,128)} %param.12) | data formatting | bytes 32768 | tf_op args[5]
  0.9 0.0 copy-done.5
  0.9 0.0 copy-done.4
  0.9 0.1 copy-done.3
  1.0 0.0 copy-start
  1.0 1.2 %copy-done = bf16[512,1024]{1,0:T(8,128)(2,1)S(1)} copy-done((bf16[512,1024]{1,0:T(8,128)(2,1)S(1)}, bf16[512,1024]{1,0:T(8,128)(2,1)}, u32[]{:S(2)}) %copy-start) | copy-done | bytes 1048600
  2.2 0.0 copy-start.1
  2.2 1.2 %copy-done.1 = bf16[512,1024]{1,0:T(8,128)(2,1)S(1)} copy-done((bf16[512,1024]{1,0:T(8,128)(2,1)S(1)}, bf16[512,1024]{1,0:T(8,128)(2,1)}, u32[]{:S(2)}) %copy-start.1) | copy-done | bytes 1048600
  3.5 0.0 copy-start.2
  3.5 1.2 %copy-done.2 = bf16[512,1024]{1,0:T(8,128)(2,1)S(1)} copy-done((bf16[512,1024]{1,0:T(8,128)(2,1)S(1)}, bf16[512,1024]{1,0:T(8,128)(2,1)}, u32[]{:S(2)}) %copy-start.2) | copy-done | bytes 1048600
  4.7 42.3 %shard_map.73 = bf16[512,1024]{1,0:T(8,128)(2,1)S(1)} custom-call(bf16[512,128]{1,0:T(8,128)(2,1)S(1)} %copy-done.3, bf16[512,128]{1,0:T(8,128)(2,1)S(1)} %copy-done.4, f32[512,8]{1,0:T(8,128)S(1)} %copy.8.gates, f32[3,1024]{1,0:T(4,128)S(1)} %copy-done.5, bf16[512,1024]{1,0:T(8,128)(2,1)S(1)} %copy-done, bf16[512,1024]{1,0:T(8,128)(2,1)S(1)} %copy-done.1, ...), custom_call_target="tpu_custom_call" | custom-call | tf_op jit(solution)/shard_map/pallas_call | solution.py:306
  47.0 1.0 %copy.10 = bf16[512,1024]{1,0:T(8,128)(2,1)} copy(bf16[512,1024]{1,0:T(8,128)(2,1)S(1)} %shard_map.73) | data formatting | bytes 2097152
Async XLA Ops:
  0.0 0.9 %copy-start.5 = (f32[3,1024]{1,0:T(4,128)S(1)}, f32[3,1024]{1,0:T(4,128)}, u32[]{:S(2)}) copy-start(f32[3,1024]{1,0:T(4,128)} %weight.1) | copy-start | bytes 36868
  0.0 0.9 %copy-start.4 = (bf16[512,128]{1,0:T(8,128)(2,1)S(1)}, bf16[512,128]{1,0:T(8,128)(2,1)}, u32[]{:S(2)}) copy-start(bf16[512,128]{1,0:T(8,128)(2,1)} %kf.1) | copy-start | bytes 393220
  0.0 1.0 %copy-start.3 = (bf16[512,128]{1,0:T(8,128)(2,1)S(1)}, bf16[512,128]{1,0:T(8,128)(2,1)}, u32[]{:S(2)}) copy-start(bf16[512,128]{1,0:T(8,128)(2,1)} %qf.1) | copy-start | bytes 393220
  1.0 1.2 %copy-start = (bf16[512,1024]{1,0:T(8,128)(2,1)S(1)}, bf16[512,1024]{1,0:T(8,128)(2,1)}, u32[]{:S(2)}) copy-start(bf16[512,1024]{1,0:T(8,128)(2,1)} %values.1) | copy-start | bytes 3145732
  2.2 1.2 %copy-start.1 = (bf16[512,1024]{1,0:T(8,128)(2,1)S(1)}, bf16[512,1024]{1,0:T(8,128)(2,1)}, u32[]{:S(2)}) copy-start(bf16[512,1024]{1,0:T(8,128)(2,1)} %win_key.1) | copy-start | bytes 3145732
  3.5 1.2 %copy-start.2 = (bf16[512,1024]{1,0:T(8,128)(2,1)S(1)}, bf16[512,1024]{1,0:T(8,128)(2,1)}, u32[]{:S(2)}) copy-start(bf16[512,1024]{1,0:T(8,128)(2,1)} %win_query.1) | copy-start | bytes 3145732

commit v2 on v1

--- a/solution.py
+++ b/solution.py
@@ -124,18 +124,17 @@
             e_send.at[source], e_recv.at[source], es_sem.at[source], er_sem.at[source],
             device_id={"seq": source}, device_id_type=MESH)
 
-    lower = jnp.where(
-        lax.broadcasted_iota(jnp.int32, (tok, tok), 0) >= lax.broadcasted_iota(jnp.int32, (tok, tok), 1),
+    before_or_at = jnp.where(
+        lax.broadcasted_iota(jnp.int32, (tok, tok), 0) <= lax.broadcasted_iota(jnp.int32, (tok, tok), 1),
         1.0, 0.0).astype(BF16)
-    wide = jnp.concatenate([gates[...], jnp.zeros((tok, 128 - heads), F32)], axis=1)
-    upper = wide.astype(BF16)
-    rest = wide - upper.astype(F32)
+    upper = gates[...].astype(BF16)
+    rest = gates[...] - upper.astype(F32)
     middle = rest.astype(BF16)
     lowest = (rest - middle.astype(F32)).astype(BF16)
-    total = dot(lower, upper) + (dot(lower, middle) + dot(lower, lowest))
-    ccol[...] = total
-    turned = total.T
-    crow[...] = turned[0:heads, :]
+    total = dot(jnp.concatenate([upper, middle, lowest], axis=0), before_or_at)
+    total = total[0:heads] + (total[heads:2 * heads] + total[2 * heads:3 * heads])
+    crow[...] = total
+    ccol[...] = jnp.concatenate([total, jnp.zeros((128 - heads, tok), F32)], axis=0).T
     kt[...] = kf[...].astype(F32).T
     qt[...] = qf[...].astype(F32).T
     keep_row = jnp.exp(crow[:, tok - 1:tok] - crow[...])
@@ -155,11 +154,11 @@
         lanes = slice(h * size, (h + 1) * size)
         phik = fold_features(kt[h * width:(h + 1) * width, :], 1.0, 1.0, 1.0)
         current = vx[tail:tail + tok, lanes].astype(F32)
-        vf[8:8 + tok, :] = current
-        vf[0:8, :] = halo[:, lanes].astype(F32)[8:16, :]
+        vf[8:8 + tok, lanes] = current
+        vf[0:8, lanes] = halo[:, lanes].astype(F32)[8:16, :]
         conv = weight[0:1, lanes] * current
         for tap in range(1, weight.shape[0]):
-            conv = conv + weight[tap:tap + 1, lanes] * vf[8 - tap:8 - tap + tok, :]
+            conv = conv + weight[tap:tap + 1, lanes] * vf[8 - tap:8 - tap + tok, lanes]
         conv = conv.astype(BF16)
         vw[h, :, 0:size] = conv
         vw[h, :, size:2 * size] = jnp.ones((tok, size), BF16)
@@ -301,7 +300,7 @@
         width = q_feat.shape[1] // heads
         rows = FOLDED * heads // n
         vmem = pl.BlockSpec(memory_space=pltpu.VMEM)
-        anywhere = pl.BlockSpec(memory_space=pl.ANY)
+        anywhere = pl.BlockSpec(memory_space=pltpu.HBM)
         dma = pltpu.SemaphoreType.DMA
         return pl.pallas_call(
             functools.partial(kernel, n, heads, size, width),
@@ -313,7 +312,7 @@
                 pltpu.VMEM((tok + WINDOW, channels), BF16),
                 pltpu.VMEM((tok, channels), BF16),
                 pltpu.VMEM((16, channels), BF16),
-                pltpu.VMEM((tok + 8, size), F32),
+                pltpu.VMEM((tok + 8, channels), F32),
                 pltpu.VMEM((heads, tok, 2 * size), BF16),
                 pltpu.VMEM((heads * width, tok), F32),
                 pltpu.VMEM((heads * width, tok), F32),
@@ -331,8 +330,8 @@
                 dma((n,)), dma((n,)), dma((n,)), dma((n,)), dma((n,)), dma((n,)),
             ],
             compiler_params=pltpu.CompilerParams(
-                collective_id=0, has_side_effects=True, vmem_limit_bytes=48 * 1024 * 1024),
-        )(q_feat, k_feat, log_gates, conv_weight, values, win_key, win_query)
+                collective_id=0, has_side_effects=True, vmem_limit_bytes=56 * 1024 * 1024),
+        )(q_feat, k_feat, log_gates.T, conv_weight, values, win_key, win_query)
 
     shard = P(("grp", "seq"), "head")
     return jax.shard_map(

time: 48.2 us -> 46.6 us (0.967)
  local copies, waits for them, and re-layouts: 5.62 us -> 2.26 us
  Pallas kernels: 42.3 us -> 44.1 us
    unnamed x14 -> x1, local copies, waits for them, and re-layouts: 5.62 us -> 2.26 us
    pallas_call x1, Pallas kernels: 42.3 us -> 44.1 us  [local(): pl.pallas_call(functools.partial(kernel, n, heads, size, width), out_shap...]
where the time goes in v2:
time: 46.6 us; the launch traced here: 46.4 us
  Pallas kernels  44.1 us (95%)
  local copies, waits for them, and re-layouts  2.26 us (5%)
    pallas_call x1, Pallas kernels, local(): pl.pallas_call(functools.partial(kernel, n, heads, size, width), out_shap...  44.1 us
    unnamed x1, local copies, waits for them, and re-layouts  2.26 us

profile of v2, /device:TPU:24, one launch (start us, length us, event | category | flops | bytes accessed | tf_op | source)
XLA Modules:
  0.0 46.4 jit_solution(9342502855966014933)
XLA Ops:
  0.0 44.1 %shard_map.73 = bf16[512,1024]{1,0:T(8,128)(2,1)} custom-call(bf16[512,128]{1,0:T(8,128)(2,1)} %qf.1, bf16[512,128]{1,0:T(8,128)(2,1)} %kf.1, f32[8,512]{1,0:T(8,128)} %bitcast.1, f32[3,1024]{1,0:T(4,128)} %weight.1, bf16[512,1024]{1,0:T(8,128)(2,1)} %values.1, bf16[512,1024]{1,0:T(8,128)(2,1)} %win_key.1, bf16[512,1024]{1,0:T(8,128)(2,1)} %win_query.1), custom_call_target="tpu_custom_call" | custom-call | tf_op jit(solution)/shard_map/pallas_call | solution.py:305
  44.1 2.3 %copy.9 = bf16[512,1024]{1,0:T(8,128)(2,1)} copy(bf16[512,1024]{1,0:T(8,128)(2,1)} %shard_map.73) | data formatting | bytes 2097152

commit v3 on v2

--- a/solution.py
+++ b/solution.py
@@ -43,7 +43,7 @@
     n, heads, size, width,
     qf, kf, gates, weight, values, win_key, win_query,
     out,
-    vx, kx, wq, halo, vf, vw, qt, kt, phiq, numden, win, ccol, crow,
+    vx, kx, wq, halo, vf, vw, qt, kt, phik, phiq, numden, win, ccol, crow,
     s_send, s_recv, side, e_send, e_recv,
     in_sem, halo_send, halo_recv, ss_sem, sr_sem, ds_sem, dr_sem, es_sem, er_sem,
 ):
@@ -72,8 +72,6 @@
         vx[0:tail, :] = jnp.zeros((tail, heads * size), BF16)
         kx[0:tail, :] = jnp.zeros((tail, heads * size), BF16)
         halo[...] = jnp.zeros(halo.shape, BF16)
-
-    pl.semaphore_wait(barrier, n - 1)
 
     nxt = lax.rem(me + 1, n)
 
@@ -88,11 +86,6 @@
             win_key.at[pl.ds(tok - tail, tail)], kx.at[pl.ds(0, tail)], halo_send.at[2], halo_recv.at[2],
             device_id={"seq": nxt}, device_id_type=MESH)
         return short, long_v, long_k
-
-    @pl.when(me < n - 1)
-    def _():
-        for copy in halo_copies():
-            copy.start()
 
     def s_copy(block):
         return pltpu.make_async_remote_copy(
@@ -142,6 +135,15 @@
     keep_lo = (keep_row - keep_hi.astype(F32)).astype(BF16)
     finish = jnp.exp(crow[:, tok - 1:tok])
 
+    pl.semaphore_wait(barrier, n - 1)
+
+    @pl.when(me < n - 1)
+    def _():
+        for copy in halo_copies():
+            copy.start()
+
+    for h in range(heads):
+        phik[h] = fold_features(kt[h * width:(h + 1) * width, :], 1.0, 1.0, 1.0)
     load_v.wait()
 
     @pl.when(me > 0)
@@ -152,7 +154,6 @@
     norm = jnp.zeros((heads, FOLDED), F32)
     for h in range(heads):
         lanes = slice(h * size, (h + 1) * size)
-        phik = fold_features(kt[h * width:(h + 1) * width, :], 1.0, 1.0, 1.0)
         current = vx[tail:tail + tok, lanes].astype(F32)
         vf[8:8 + tok, lanes] = current
         vf[0:8, lanes] = halo[:, lanes].astype(F32)[8:16, :]
@@ -164,26 +165,21 @@
         vw[h, :, size:2 * size] = jnp.ones((tok, size), BF16)
         column = ccol[:, h:h + 1]
         keep = jnp.exp(ccol[tok - 1:tok, h:h + 1] - column)
-        state = dot(phik, (conv.astype(F32) * keep).astype(BF16))
-        norm_h = dot_t(keep_hi, phik) + dot_t(keep_lo, phik)
+        state = dot(phik[h], (conv.astype(F32) * keep).astype(BF16))
+        norm_h = dot_t(keep_hi, phik[h]) + dot_t(keep_lo, phik[h])
         norm = jnp.where(head_row == h, norm_h, norm)
         for b in range(per_head):
             block = h * per_head + b
-            piece = state[b * rows:(b + 1) * rows, :].astype(BF16)
-
-            @pl.when(block != me)
-            def _(block=block, piece=piece):
-                s_send[block] = piece
-                s_copy(block).start()
-
-            @pl.when(block == me)
-            def _(piece=piece):
-                s_recv[me] = piece
-
+            s_send[block] = state[b * rows:(b + 1) * rows, :].astype(BF16)
+
+    s_recv[me] = s_send[me]
     side[me] = jnp.concatenate([norm, jnp.broadcast_to(finish, (heads, 256 - FOLDED))], axis=1)
-    for peer in range(n):
-        @pl.when(peer != me)
-        def _(peer=peer):
+
+    @pl.when(me < n - 1)
+    def _():
+        for offset in range(1, n):
+            peer = lax.rem(me + offset, n)
+            s_copy(peer).start()
             d_copy(peer).start()
 
     lane_head = lax.broadcasted_iota(jnp.int32, (tok, heads * width), 1) // width
@@ -207,7 +203,41 @@
             score = (poly * jnp.exp(gap)).astype(BF16)
             numden[h, t0:reach, :] = dot(score, vw[h, 0:reach, :])
 
-    for source in range(n):
+    load_k.wait()
+    load_q.wait()
+
+    @pl.when(me > 0)
+    def _():
+        halo_copies()[1].wait_recv()
+        halo_copies()[2].wait_recv()
+
+    r = lax.broadcasted_iota(jnp.int32, (WINDOW, 2 * WINDOW), 0)
+    j = lax.broadcasted_iota(jnp.int32, (WINDOW, 2 * WINDOW), 1)
+    band = (j > r) & (j <= r + WINDOW)
+    steps = tok // WINDOW
+    bias = jnp.where(band, 0.0, -1e30)
+    bias = jnp.concatenate(
+        [jnp.where(band & ((j >= WINDOW) | (me > 0)), 0.0, -1e30)] + [bias] * (steps - 1), axis=0)
+    scale = size ** (-0.5)
+    ones = jnp.ones((2 * WINDOW, size), BF16)
+
+    def slide(h):
+        lanes = slice(h * size, (h + 1) * size)
+        s = jnp.concatenate([
+            dot_t(wq[i * WINDOW:(i + 1) * WINDOW, lanes], kx[i * WINDOW:(i + 2) * WINDOW, lanes])
+            for i in range(steps)], axis=0)
+        s = s * scale + bias
+        p = jnp.exp(s - jnp.max(s, axis=1, keepdims=True)).astype(BF16)
+        pv = jnp.concatenate([
+            dot(p[i * WINDOW:(i + 1) * WINDOW, :],
+                jnp.concatenate([vx[i * WINDOW:(i + 2) * WINDOW, lanes], ones], axis=1))
+            for i in range(steps)], axis=0)
+        win[:, lanes] = pv[:, 0:size] / pv[:, size:2 * size]
+
+    for h in range(heads // 2):
+        slide(h)
+
+    for source in range(n - 1):
         @pl.when(source != me)
         def _(source=source):
             s_arrival(source).wait_recv()
@@ -215,57 +245,39 @@
 
     mine = me // per_head
     running = jnp.zeros((rows, size), F32)
-    for i in range(n):
-        narrow = running.astype(BF16)
-
-        @pl.when(i != me)
-        def _(i=i, narrow=narrow):
-            e_send[i] = narrow
-            e_copy(i).start()
-
-        @pl.when(i == me)
-        def _(narrow=narrow):
-            e_recv[me] = narrow
-
+    e_send[0] = running.astype(BF16)
+    for i in range(n - 1):
         fade = side[i, pl.ds(mine, 1), :][:, 192:193]
         running = fade * running + s_recv[i].astype(F32)
+        e_send[i + 1] = running.astype(BF16)
+
+    e_recv[me] = e_send[me]
+    for offset in range(1, n):
+        peer = lax.rem(me + offset, n)
+
+        @pl.when(peer > 0)
+        def _(peer=peer):
+            e_copy(peer).start()
+
+    @pl.when(me == 0)
+    def _():
+        e_recv[...] = jnp.zeros(e_recv.shape, BF16)
 
     norm_before = jnp.zeros((heads, 256), F32)
-    for i in range(n):
+    for i in range(n - 1):
         block = side[i]
         joined = block[:, 192:193] * norm_before + block
         norm_before = jnp.where(i < me, joined, norm_before)
     norm_col = jnp.concatenate([norm_before, jnp.zeros((128 - heads, 256), F32)], axis=0).T
 
-    load_k.wait()
-    load_q.wait()
-
-    @pl.when(me > 0)
-    def _():
-        halo_copies()[1].wait_recv()
-        halo_copies()[2].wait_recv()
-
-    r = lax.broadcasted_iota(jnp.int32, (WINDOW, 2 * WINDOW), 0)
-    j = lax.broadcasted_iota(jnp.int32, (WINDOW, 2 * WINDOW), 1)
-    band = (j > r) & (j <= r + WINDOW)
-    first = band & ((j >= WINDOW) | (me > 0))
-    scale = size ** (-0.5)
-    ones = jnp.ones((2 * WINDOW, size), BF16)
-    for h in range(heads):
-        lanes = slice(h * size, (h + 1) * size)
-        for i in range(tok // WINDOW):
-            t0 = i * WINDOW
-            s = dot_t(wq[t0:t0 + WINDOW, lanes], kx[t0:t0 + 2 * WINDOW, lanes]) * scale
-            s = jnp.where(first if i == 0 else band, s, -1e30)
-            p = jnp.exp(s - jnp.max(s, axis=1, keepdims=True)).astype(BF16)
-            pv = dot(p, jnp.concatenate([vx[t0:t0 + 2 * WINDOW, lanes], ones], axis=1))
-            win[t0:t0 + WINDOW, lanes] = pv[:, 0:size] / pv[:, size:2 * size]
+    for h in range(heads // 2, heads):
+        slide(h)
 
     for h in range(heads):
         phiq[h] = fold_features(qt[h * width:(h + 1) * width, :], 1.0 / 32, 1.0 / 16, 0.25)
 
     for source in range(n):
-        @pl.when(source != me)
+        @pl.when((source != me) & (me > 0))
         def _(source=source):
             e_arrival(source).wait_recv()
 
@@ -283,11 +295,15 @@
             copy.wait_send()
 
     for peer in range(n):
-        @pl.when(peer != me)
+        @pl.when((peer != me) & (me < n - 1))
         def _(peer=peer):
             s_copy(peer).wait_send()
             d_copy(peer).wait_send()
-            e_copy(peer).wait_send()
+
+        if peer > 0:
+            @pl.when(peer != me)
+            def _(peer=peer):
+                e_copy(peer).wait_send()
 
 
 def solution(mesh):
@@ -317,6 +333,7 @@
                 pltpu.VMEM((heads * width, tok), F32),
                 pltpu.VMEM((heads * width, tok), F32),
                 pltpu.VMEM((heads, FOLDED, tok), BF16),
+                pltpu.VMEM((heads, FOLDED, tok), BF16),
                 pltpu.VMEM((heads, tok, 2 * size), F32),
                 pltpu.VMEM((tok, channels), F32),
                 pltpu.VMEM((tok, 128), F32),
@@ -330,7 +347,7 @@
                 dma((n,)), dma((n,)), dma((n,)), dma((n,)), dma((n,)), dma((n,)),
             ],
             compiler_params=pltpu.CompilerParams(
-                collective_id=0, has_side_effects=True, vmem_limit_bytes=56 * 1024 * 1024),
+                collective_id=0, has_side_effects=True, vmem_limit_bytes=32 * 1024 * 1024),
         )(q_feat, k_feat, log_gates.T, conv_weight, values, win_key, win_query)
 
     shard = P(("grp", "seq"), "head")

time: 46.6 us -> 37.8 us (0.81)
  the two profiles are of different devices: /device:TPU:24 before, /device:TPU:10 now
where the time goes in v3:
time: 37.8 us; the launch traced here: 37.4 us
  Pallas kernels  29.5 us (78%)
  local copies, waits for them, and re-layouts  7.89 us (21%)
    pallas_call x1, Pallas kernels, local(): pl.pallas_call(functools.partial(kernel, n, heads, size, width), out_shap...  29.5 us
    unnamed x15, local copies, waits for them, and re-layouts  7.89 us

profile of v3, /device:TPU:10, one launch (start us, length us, event | category | flops | bytes accessed | tf_op | source)
XLA Modules:
  0.0 37.4 jit_solution(575396853845497533)
XLA Ops:
  0.0 0.0 copy-start
  0.0 1.2 %copy-done = bf16[512,1024]{1,0:T(8,128)(2,1)S(1)} copy-done((bf16[512,1024]{1,0:T(8,128)(2,1)S(1)}, bf16[512,1024]{1,0:T(8,128)(2,1)}, u32[]{:S(2)}) %copy-start) | copy-done | bytes 1048600
  1.2 0.0 copy-start.1
  1.2 1.2 %copy-done.1 = bf16[512,1024]{1,0:T(8,128)(2,1)S(1)} copy-done((bf16[512,1024]{1,0:T(8,128)(2,1)S(1)}, bf16[512,1024]{1,0:T(8,128)(2,1)}, u32[]{:S(2)}) %copy-start.1) | copy-done | bytes 1048600
  2.5 0.0 copy-start.2
  2.5 1.2 %copy-done.2 = bf16[512,1024]{1,0:T(8,128)(2,1)S(1)} copy-done((bf16[512,1024]{1,0:T(8,128)(2,1)S(1)}, bf16[512,1024]{1,0:T(8,128)(2,1)}, u32[]{:S(2)}) %copy-start.2) | copy-done | bytes 1048600
  3.7 0.0 copy-start.3
  3.7 0.9 %copy-done.3 = bf16[512,128]{1,0:T(8,128)(2,1)S(1)} copy-done((bf16[512,128]{1,0:T(8,128)(2,1)S(1)}, bf16[512,128]{1,0:T(8,128)(2,1)}, u32[]{:S(2)}) %copy-start.3) | copy-done | bytes 131096
  4.6 0.0 copy-start.4
  4.6 0.9 %copy-done.4 = bf16[512,128]{1,0:T(8,128)(2,1)S(1)} copy-done((bf16[512,128]{1,0:T(8,128)(2,1)S(1)}, bf16[512,128]{1,0:T(8,128)(2,1)}, u32[]{:S(2)}) %copy-start.4) | copy-done | bytes 131096
  5.5 0.0 copy-start.5
  5.5 0.7 %copy-done.5 = f32[512,8]{0,1:T(8,128)S(1)} copy-done((f32[512,8]{0,1:T(8,128)S(1)}, f32[512,8]{0,1:T(8,128)}, u32[]{:S(2)}) %copy-start.5) | copy-done | bytes 16408
  6.2 0.0 copy-start.6
  6.2 0.7 %copy-done.6 = f32[3,1024]{1,0:T(4,128)S(1)} copy-done((f32[3,1024]{1,0:T(4,128)S(1)}, f32[3,1024]{1,0:T(4,128)}, u32[]{:S(2)}) %copy-start.6) | copy-done | bytes 12312
  6.9 29.5 %shard_map.73 = bf16[512,1024]{1,0:T(8,128)(2,1)S(1)} custom-call(bf16[512,128]{1,0:T(8,128)(2,1)S(1)} %copy-done.3, bf16[512,128]{1,0:T(8,128)(2,1)S(1)} %copy-done.4, f32[8,512]{1,0:T(8,128)S(1)} %bitcast.1, f32[3,1024]{1,0:T(4,128)S(1)} %copy-done.6, bf16[512,1024]{1,0:T(8,128)(2,1)S(1)} %copy-done, bf16[512,1024]{1,0:T(8,128)(2,1)S(1)} %copy-done.1, ...), custom_call_target="tpu_custom_call" | custom-call | tf_op jit(solution)/shard_map/pallas_call | solution.py:321
  36.5 1.0 %copy.9 = bf16[512,1024]{1,0:T(8,128)(2,1)} copy(bf16[512,1024]{1,0:T(8,128)(2,1)S(1)} %shard_map.73) | data formatting | bytes 2097152
Async XLA Ops:
  0.0 1.2 %copy-start = (bf16[512,1024]{1,0:T(8,128)(2,1)S(1)}, bf16[512,1024]{1,0:T(8,128)(2,1)}, u32[]{:S(2)}) copy-start(bf16[512,1024]{1,0:T(8,128)(2,1)} %values.1) | copy-start | bytes 3145732
  1.2 1.2 %copy-start.1 = (bf16[512,1024]{1,0:T(8,128)(2,1)S(1)}, bf16[512,1024]{1,0:T(8,128)(2,1)}, u32[]{:S(2)}) copy-start(bf16[512,1024]{1,0:T(8,128)(2,1)} %win_key.1) | copy-start | bytes 3145732
  2.5 1.2 %copy-start.2 = (bf16[512,1024]{1,0:T(8,128)(2,1)S(1)}, bf16[512,1024]{1,0:T(8,128)(2,1)}, u32[]{:S(2)}) copy-start(bf16[512,1024]{1,0:T(8,128)(2,1)} %win_query.1) | copy-start | bytes 3145732
  3.7 0.9 %copy-start.3 = (bf16[512,128]{1,0:T(8,128)(2,1)S(1)}, bf16[512,128]{1,0:T(8,128)(2,1)}, u32[]{:S(2)}) copy-start(bf16[512,128]{1,0:T(8,128)(2,1)} %qf.1) | copy-start | bytes 393220
  4.6 0.9 %copy-start.4 = (bf16[512,128]{1,0:T(8,128)(2,1)S(1)}, bf16[512,128]{1,0:T(8,128)(2,1)}, u32[]{:S(2)}) copy-start(bf16[512,128]{1,0:T(8,128)(2,1)} %kf.1) | copy-start | bytes 393220
  5.5 0.7 %copy-start.5 = (f32[512,8]{0,1:T(8,128)S(1)}, f32[512,8]{0,1:T(8,128)}, u32[]{:S(2)}) copy-start(f32[512,8]{0,1:T(8,128)} %param.12) | copy-start | bytes 49156
  6.2 0.7 %copy-start.6 = (f32[3,1024]{1,0:T(4,128)S(1)}, f32[3,1024]{1,0:T(4,128)}, u32[]{:S(2)}) copy-start(f32[3,1024]{1,0:T(4,128)} %weight.1) | copy-start | bytes 36868

commit v4 on v3

--- a/solution.py
+++ b/solution.py
@@ -347,7 +347,7 @@
                 dma((n,)), dma((n,)), dma((n,)), dma((n,)), dma((n,)), dma((n,)),
             ],
             compiler_params=pltpu.CompilerParams(
-                collective_id=0, has_side_effects=True, vmem_limit_bytes=32 * 1024 * 1024),
+                collective_id=0, has_side_effects=True, vmem_limit_bytes=54 * 1024 * 1024),
         )(q_feat, k_feat, log_gates.T, conv_weight, values, win_key, win_query)
 
     shard = P(("grp", "seq"), "head")

time: 37.8 us -> 33.9 us (0.90)
  local copies, waits for them, and re-layouts: 7.89 us -> 2.26 us
  Pallas kernels: 29.5 us -> 31.4 us
    unnamed x15 -> x1, local copies, waits for them, and re-layouts: 7.89 us -> 2.26 us
    pallas_call x1, Pallas kernels: 29.5 us -> 31.4 us  [local(): pl.pallas_call(functools.partial(kernel, n, heads, size, width), out_shap...]
where the time goes in v4:
time: 33.9 us; the launch traced here: 33.7 us
  Pallas kernels  31.4 us (93%)
  local copies, waits for them, and re-layouts  2.26 us (7%)
    pallas_call x1, Pallas kernels, local(): pl.pallas_call(functools.partial(kernel, n, heads, size, width), out_shap...  31.4 us
    unnamed x1, local copies, waits for them, and re-layouts  2.26 us

profile of v4, /device:TPU:10, one launch (start us, length us, event | category | flops | bytes accessed | tf_op | source)
XLA Modules:
  0.0 33.7 jit_solution(17505543593819273944)
XLA Ops:
  0.0 31.4 %shard_map.73 = bf16[512,1024]{1,0:T(8,128)(2,1)} custom-call(bf16[512,128]{1,0:T(8,128)(2,1)} %qf.1, bf16[512,128]{1,0:T(8,128)(2,1)} %kf.1, f32[8,512]{1,0:T(8,128)} %bitcast.1, f32[3,1024]{1,0:T(4,128)} %weight.1, bf16[512,1024]{1,0:T(8,128)(2,1)} %values.1, bf16[512,1024]{1,0:T(8,128)(2,1)} %win_key.1, bf16[512,1024]{1,0:T(8,128)(2,1)} %win_query.1), custom_call_target="tpu_custom_call" | custom-call | tf_op jit(solution)/shard_map/pallas_call | solution.py:321
  31.4 2.3 %copy.9 = bf16[512,1024]{1,0:T(8,128)(2,1)} copy(bf16[512,1024]{1,0:T(8,128)(2,1)} %shard_map.73) | data formatting | bytes 2097152

commit v5 on v4

--- a/solution.py
+++ b/solution.py
@@ -171,16 +171,24 @@
         for b in range(per_head):
             block = h * per_head + b
             s_send[block] = state[b * rows:(b + 1) * rows, :].astype(BF16)
+        if h + 1 in (heads // 2, heads):
+            half = n // 2
+            start = 0 if h + 1 == heads // 2 else half
+            for turn in range(half):
+                peer = start + lax.rem(me + turn, half)
+
+                @pl.when((peer != me) & (me < n - 1))
+                def _(peer=peer):
+                    s_copy(peer).start()
+
+    side[me] = jnp.concatenate([norm, jnp.broadcast_to(finish, (heads, 256 - FOLDED))], axis=1)
+
+    @pl.when(me < n - 1)
+    def _():
+        for offset in range(1, n):
+            d_copy(lax.rem(me + offset, n)).start()
 
     s_recv[me] = s_send[me]
-    side[me] = jnp.concatenate([norm, jnp.broadcast_to(finish, (heads, 256 - FOLDED))], axis=1)
-
-    @pl.when(me < n - 1)
-    def _():
-        for offset in range(1, n):
-            peer = lax.rem(me + offset, n)
-            s_copy(peer).start()
-            d_copy(peer).start()
 
     lane_head = lax.broadcasted_iota(jnp.int32, (tok, heads * width), 1) // width
     kt_narrow = kt[...].astype(BF16)

time: 33.9 us -> 32.2 us (0.950)
  the two profiles are of different devices: /device:TPU:10 before, /device:TPU:24 now
where the time goes in v5:
time: 32.2 us; the launch traced here: 32.1 us
  Pallas kernels  29.8 us (93%)
  local copies, waits for them, and re-layouts  2.26 us (7%)
    pallas_call x1, Pallas kernels, local(): pl.pallas_call(functools.partial(kernel, n, heads, size, width), out_shap...  29.8 us
    unnamed x1, local copies, waits for them, and re-layouts  2.26 us

profile of v5, /device:TPU:24, one launch (start us, length us, event | category | flops | bytes accessed | tf_op | source)
XLA Modules:
  0.0 32.1 jit_solution(8395449810409693000)
XLA Ops:
  0.0 29.8 %shard_map.73 = bf16[512,1024]{1,0:T(8,128)(2,1)} custom-call(bf16[512,128]{1,0:T(8,128)(2,1)} %qf.1, bf16[512,128]{1,0:T(8,128)(2,1)} %kf.1, f32[8,512]{1,0:T(8,128)} %bitcast.1, f32[3,1024]{1,0:T(4,128)} %weight.1, bf16[512,1024]{1,0:T(8,128)(2,1)} %values.1, bf16[512,1024]{1,0:T(8,128)(2,1)} %win_key.1, bf16[512,1024]{1,0:T(8,128)(2,1)} %win_query.1), custom_call_target="tpu_custom_call" | custom-call | tf_op jit(solution)/shard_map/pallas_call | solution.py:329
  29.8 2.3 %copy.9 = bf16[512,1024]{1,0:T(8,128)(2,1)} copy(bf16[512,1024]{1,0:T(8,128)(2,1)} %shard_map.73) | data formatting | bytes 2097152
